TPU v7x, 512 devices: a whole 4x4x16 slice. The times are simulated.
512 devices in a mesh: img: 16 (over z_hi, y, core), term: 32 (over z_lo, x).
Axes of the slice: x: 4, y: 4, z: 16 (z_hi: 2, z_lo: 8; z = z_hi * 8 + z_lo), core: 2. Of those that a mesh axis runs over, the one named last changes fastest.
Arguments:
- patches: bfloat16 [64, 256, 1024], P('img', 'term'), may hold values from -6 to 6
- patch_mask: int32 [64, 256], P('img', 'term'), may hold values 0 or 1
- proj_weight: bfloat16 [1024, 30720], P('img', 'term'), may hold values from -0.1875 to 0.1875
- proj_bias: float32 [30720], P('term'), may hold values from -4 to 4
- slab: bfloat16 [8128, 30720], P('img', 'term'), may hold values from 0 to 2
- query_ids: int32 [1024, 32], replicated, may hold values from -1 to 30719, as said below
- term_weights: bfloat16 [1024, 32], replicated, may hold values from 0.25 to 4
Outputs:
- scores: float32 [1024, 8192], P('term', 'img')
Inputs may be any that keep to these rules, and one draw needn't show every extreme that they name: `query_ids`: within a query the non-negative ids are distinct and come before the padding slots; every query has at least 8 real terms and some query fills all 32 slots.
All inputs are finite; a program needn't handle non-finite values. No bound on the sum of `patch_mask` on one device may be relied on, other than what follows from the above.
Results may differ from a plain program's by a relative error of at most 0.0003.
Values may be sent and summed in bfloat16 or wider, within the bound.
A program may use at most 64 MiB of HBM per device.

v0:
```python
import jax
import jax.numpy as jnp
from jax import lax
from jax.sharding import PartitionSpec as P


def shards(patches, patch_mask, proj_weight, proj_bias, slab, query_ids, term_weights):
    proj_full = lax.all_gather(proj_weight, "img", axis=0, tiled=True)
    block_width = proj_full.shape[1]
    start_max = jnp.zeros((patches.shape[0], block_width), jnp.float32)
    features = lax.all_gather(patches, "term", axis=1, tiled=True)
    keep_mask = lax.all_gather(patch_mask.astype(jnp.bfloat16), "term", axis=1, tiled=True)
    logits = (
        jnp.einsum("npd,dv->npv", features, proj_full, preferred_element_type=jnp.float32)
        + proj_bias
    )
    activity = jnp.log1p(jnp.maximum(logits, 0.0))
    activity = jnp.where(keep_mask[:, :, None] > 0, activity, 0.0)
    pooled = jnp.maximum(start_max, jnp.max(activity, axis=1))
    impacts = jnp.concatenate([slab, pooled.astype(jnp.bfloat16)], axis=0)
    zero_value = jnp.zeros((), jnp.bfloat16)
    weights = jnp.where(query_ids >= 0, term_weights, zero_value)
    offset = lax.axis_index("term") * block_width
    columns = offset + lax.iota(jnp.int32, block_width)
    dense_rows = jnp.sum(
        jnp.where(query_ids[:, :, None] == columns[None, None, :], weights[:, :, None], zero_value),
        axis=1,
    )
    return lax.psum_scatter(
        lax.dot_general(
            dense_rows, impacts, (((1,), (1,)), ((), ())), preferred_element_type=jnp.float32
        ),
        "term",
        scatter_dimension=0,
        tiled=True,
    )


def solution(mesh):
    placed = (
        P("img", "term", None),
        P("img", "term"),
        P("img", "term"),
        P("term"),
        P("img", "term"),
        P(),
        P(),
    )
    return jax.shard_map(
        shards, mesh=mesh, in_specs=placed, out_specs=P("term", "img"), check_vma=False
    )
```

profile of v0, /device:TPU:24, one launch (start us, length us, event | category | flops | bytes accessed | tf_op | source)
XLA Modules:
  0.0 582.1 jit_solution(16606816592213149012)
XLA Ops:
  6.5 0.0 copy-start.1
  6.5 0.0 all-gather.6.cloned.1.call-start
  6.5 0.7 all-gather.6.cloned.1.call-update
  7.3 0.0 all-gather.4.cloned.1.call-start
  7.3 0.7 all-gather.4.cloned.1.call-update
  8.0 0.0 reduce-scatter.2.cloned.1.call-start
  8.1 0.7 convert_bitcast_fusion
  8.7 132.7 %all-gather = bf16[32,8,4]{1,2,0:T(4,128)(2,1)S(1)} all-gather(bf16[1,8,4]{1,2,0:T(4,128)(2,1)S(1)} %convert_bitcast_fusion), channel_id=1, replica_groups=mesh['img'=16,'term'=32] {'term'}, dimensions={0}, use_global_device_ids=true | all-gather | bytes 2112 | tf_op jit(solution)/shard_map/all_gather | solution.py:12
  141.4 0.1 copy.23
  141.5 0.1 copy.24
  141.6 0.1 reshape.12
  141.7 1.0 compare_select_fusion.1
  142.7 17.3 %fusion = bf16[1024,960]{0,1:T(8,128)(2,1)S(1)} fusion(s32[1024,32]{0,1:T(8,128)} %param.12, s32[960]{0:T(1024)S(1)} %iota_add_fusion, bf16[1024,32]{0,1:T(8,128)(2,1)S(1)} %compare_select_fusion.1), kind=kLoop, calls=%fused_computation.1 | loop fusion | flops 93388800 | bytes 2166528 | tf_op jit(solution)/shard_map/reduce_sum | solution.py:25
  160.1 0.0 all-gather.6.cloned.1.call-done
  160.1 163.3 %all-gather.4.cloned.1.call-done = bf16[4,256,1024]{2,1,0:T(8,128)(2,1)} async-done(((bf16[4,8,1024]{2,1,0:T(8,128)(2,1)}), bf16[4,256,1024]{2,1,0:T(8,128)(2,1)}) %all-gather.4.cloned.1.call-update) | async-done | bytes 2097168 | tf_op jit(solution)/shard_map/all_gather | solution.py:11
  323.4 0.0 copy-done.1
  323.4 0.0 copy-start
  323.4 6.1 %select_reduce_fusion = bf16[4,960]{1,0:T(4,128)(2,1)S(1)} fusion(f32[960]{0:T(1024)S(1)} %copy-done.1, pred[4,256]{1,0:T(4,128)(4,1)S(1)} %bitcast.14, bf16[4,256,1024]{2,1,0:T(8,128)(2,1)} %all-gather.4.cloned.1.call-done, bf16[1024,960]{1,0:T(8,128)(2,1)} %all-gather.6.cloned.1.call-done), kind=kOutput, calls=%fused_computation.2 | convolution fusion | flops 2017194240 | bytes 4075776 | tf_op jit(solution)/shard_map/npd,dv->npv/dot_general | solution.py:14
  329.5 0.2 copy.25
  329.7 0.0 copy-done
  329.8 2.7 fusion.5
  332.4 0.0 reduce-scatter.2.cloned.1.call-update
  332.5 243.2 %reduce-scatter.2.cloned.1.call-done = f32[32,512]{1,0:T(8,128)} async-done(((f32[1024,512]{1,0:T(8,128)}), f32[32,512]{1,0:T(8,128)}) %reduce-scatter.2.cloned.1.call-update) | async-done | bytes 65552 | tf_op jit(solution)/shard_map/reduce_scatter | solution.py:29
  (3 shorter events, 0.0 us)
Async XLA Ops:
  6.5 316.8 %copy-start.1 = (f32[960]{0:T(1024)S(1)}, f32[960]{0:T(1024)}, u32[]{:S(2)}) copy-start(f32[960]{0:T(1024)} %param.10) | copy-start | bytes 11524
  6.5 153.5 %all-gather.6.cloned.1.call-start = ((), (), s32[]{:S(2)}) async-start(), calls=%async_computation.2 | async-start | bytes 2228224 | tf_op jit(solution)/shard_map/all_gather | solution.py:8
  7.3 316.1 %all-gather.4.cloned.1.call-start = ((), (), s32[]{:S(2)}) async-start(), calls=%async_computation.1 | async-start | bytes 2162688 | tf_op jit(solution)/shard_map/all_gather | solution.py:11
  8.0 567.6 %reduce-scatter.2.cloned.1.call-start = ((), (), s32[]{:S(2)}) async-start(), calls=%async_computation.3 | async-start | bytes 2162688 | tf_op jit(solution)/shard_map/reduce_scatter | solution.py:29
  323.4 6.4 %copy-start = (bf16[508,960]{0,1:T(8,128)(2,1)S(1)}, bf16[508,960]{0,1:T(8,128)(2,1)}, u32[]{:S(2)}) copy-start(bf16[508,960]{0,1:T(8,128)(2,1)} %param.11) | copy-start | bytes 2926084
Sparse Core Ops, SparseCore 0:
  10.6 95.9 all-gather.5
  108.7 214.5 all-gather.3
  332.6 242.9 reduce-scatter.1
where the time goes:
time: 582 us
  waiting for transfers between devices  408 us (70%)
  blocking collectives  133 us (23%)
  other arithmetic  19 us (3%)
  between operations  13.2 us (2%)
  matrix products  8.82 us (2%)
    reduce_scatter x1, waiting for transfers between devices, shards(): lax.psum_scatter(lax.dot_general(dense_rows, impacts, (((1,), (1,)), ((),...  243 us
    all_gather x1, waiting for transfers between devices, shards(): features = lax.all_gather(patches, 'term', axis=1, tiled=True)  163 us
    all_gather x1, blocking collectives, shards(): lax.all_gather(patch_mask.astype(jnp.bfloat16), 'term', axis=1, tiled=True)  133 us
    reduce_sum x1, other arithmetic, shards(): jnp.sum(jnp.where(query_ids[:, :, None] == columns[None, None, :], weight...  17.3 us
  transfers between devices with their start and end apart: 3, of which 2 were waited for; matrix products, arithmetic and copies ran while one was open for 3% of the time, Pallas kernels for 0%

commit v1 on v0

v1 whole, which is shorter than its diff:
```python
import functools

import jax
import jax.numpy as jnp
from jax import lax
from jax.experimental import pallas as pl
from jax.experimental.pallas import tpu as pltpu
from jax.sharding import PartitionSpec as P

MESH = pl.DeviceIdType.MESH
NX, NY, NZ, NH = 4, 4, 8, 2
EXTRA = 128
FAR = (4, 3, 5, 2, 6, 1, 7, 0)
MASKED = -1e30


def remote(src, dst, send, recv, **where):
    return pltpu.make_async_remote_copy(
        src_ref=src, dst_ref=dst, send_sem=send, recv_sem=recv, device_id=where, device_id_type=MESH
    )


def kernel(
    ids_ref, tw_ref, bias_ref, pat_ref, wt_ref, slab_ref,
    main_ref, new_ref,
    feats, weight, dense, part, half_in, full_in, z_in, relay, runmax, fresh, fresh_x, fresh_z, fresh_in,
    zs, zr, xs, xr, hs, hr, rs, rr, ws, wr, ys, yr, cs, cr,
    as_, ar, bs, br, qs, qr, tx_s, tx_r, tz_s, tz_r,
):
    img = lax.axis_index("img")
    term = lax.axis_index("term")
    core, y, zh = lax.rem(img, 2), lax.rem(lax.div(img, 2), NY), lax.div(img, 2 * NY)
    x, zl = lax.rem(term, NX), lax.div(term, NX)

    def at_x(d):
        return zl * NX + lax.rem(x + d, NX)

    def at_zl(k):
        return k * NX + x

    def at_y(d):
        return zh * 8 + lax.rem(y + d, NY) * 2 + core

    def at_z(d):
        far = lax.rem(zh * NZ + zl + d, NH * NZ)
        return {"img": lax.div(far, NZ) * 8 + y * 2 + core, "term": lax.rem(far, NZ) * NX + x}

    partner = zh * 8 + y * 2 + 1 - core
    out_of_line = at_z(jnp.where(zl < 4, 12, 4))

    barrier = pltpu.get_barrier_semaphore()
    for d in range(1, NZ):
        pl.semaphore_signal(barrier, inc=1, device_id={"term": at_zl(lax.rem(zl + d, NZ))}, device_id_type=MESH)
    pl.semaphore_signal(barrier, inc=1, device_id=out_of_line, device_id_type=MESH)
    for d in range(1, NX):
        pl.semaphore_signal(barrier, inc=1, device_id={"term": at_x(d)}, device_id_type=MESH)
    for d in range(1, NY):
        pl.semaphore_signal(barrier, inc=1, device_id={"img": at_y(d)}, device_id_type=MESH)
    pl.semaphore_signal(barrier, inc=1, device_id={"img": partner}, device_id_type=MESH)

    width = dense.shape[1]
    first = term * width

    def chunk(k):
        c = lax.rem(zl + FAR[k], NZ)

        def rows16(r, carry):
            rows = pl.ds(pl.multiple_of(c * 128 + r * 16, 16), 16)
            ids = ids_ref[rows, :] - first
            tw = tw_ref[rows, :].astype(jnp.float32)
            lane = lax.broadcasted_iota(jnp.int32, (16, width), 1)
            acc = jnp.zeros((16, width), jnp.float32)
            for j in range(ids.shape[1]):
                acc = jnp.where(ids[:, j : j + 1] == lane, tw[:, j : j + 1], acc)
            dense[rows, :] = acc.astype(jnp.bfloat16)
            return carry

        lax.fori_loop(0, 8, rows16, 0)
        share = lax.dot_general(
            dense[pl.ds(pl.multiple_of(c * 128, 128), 128), :], slab_ref[...],
            (((1,), (1,)), ((), ())), preferred_element_type=jnp.float32,
        )
        stored = slab_ref.shape[0]
        for d in range(NX):
            part[c, d, :, 384:512] = jnp.zeros((32, 128), jnp.float32)
            part[c, d, :, 0:stored] = share[d * 32 : (d + 1) * 32, :]

    chunk(0)
    pl.semaphore_wait(barrier, 15)

    def block(o):
        return pat_ref if o is None else feats.at[x, o]

    def z_right(src, o):
        return remote(src, feats.at[x, o], zs.at[0, o], zr.at[o], term=at_zl(zl + 1))

    def z_left(src, o):
        return remote(src, feats.at[x, o], zs.at[1, o], zr.at[o], term=at_zl(zl - 1))

    def x_send(src, o, way):
        return remote(src, feats.at[x, o], xs.at[way, o], xr.at[way, o], term=at_x((1, 3)[way]))

    def x_forward(o, way):
        owner = lax.rem(x + (3, 1)[way], NX)
        rows = pl.ds(way * 16, 16)
        return remote(
            feats.at[owner, o, rows], feats.at[owner, o, rows], hs.at[way, o], hr.at[way, o], term=at_x((1, 3)[way])
        )

    def x_take(o, way):
        owner = lax.rem(x + (3, 1)[way], NX)
        remote(feats.at[owner, o], feats.at[owner, o], xs.at[way, o], xr.at[way, o], term=at_x((1, 3)[way])).wait_recv()

    def half_take(o, way):
        owner = lax.rem(x + 2, NX)
        rows = pl.ds(way * 16, 16)
        remote(
            feats.at[owner, o, rows], feats.at[owner, o, rows], hs.at[way, o], hr.at[way, o], term=at_x((1, 3)[way])
        ).wait_recv()

    def spread(src, o):
        x_send(src, o, 0).start()
        x_send(src, o, 1).start()

    def pass_on(o):
        for way in (0, 1):
            x_take(o, way)
            x_forward(o, way).start()

    def rows_of(h, yy, cc, lo=0, n=64):
        return weight.at[pl.ds(pl.multiple_of((h * 8 + yy * 2 + cc) * 64 + lo, 32), n)]

    def relay_send(way):
        return remote(wt_ref.at[pl.ds(way * 32, 32)], relay.at[way], rs.at[way], rr.at[way], **at_z((4, 12)[way]))

    def relay_on(way):
        far = at_z((4, 12)[way])
        h = lax.div(far["img"], 8)
        dst = rows_of(1 - h, y, core, way * 32, 32)
        return remote(relay.at[way], dst, ws.at[way], wr.at[way], **far)

    def relay_take(way):
        far = at_z((4, 12)[way])
        dst = rows_of(1 - zh, y, core, way * 32, 32)
        remote(relay.at[way], dst, ws.at[way], wr.at[way], **far).wait_recv()

    def y_send(b, d):
        src = wt_ref if b == 0 else rows_of(1 - zh, y, core)
        h = zh if b == 0 else 1 - zh
        return remote(src, rows_of(h, y, core), ys.at[b, d - 1], yr.at[b, d - 1], img=at_y(d))

    def y_take(b, d):
        h = zh if b == 0 else 1 - zh
        dst = rows_of(h, lax.rem(y + NY - d, NY), core)
        remote(dst, dst, ys.at[b, d - 1], yr.at[b, d - 1], img=at_y(d)).wait_recv()

    def c_send(b, d):
        h = zh if b == 0 else 1 - zh
        dst = rows_of(h, lax.rem(y + NY - d, NY), core)
        src = wt_ref if (b == 0 and d == 0) else dst
        return remote(src, dst, cs.at[b, d], cr.at[b, d], img=partner)

    def c_take(b, d):
        h = zh if b == 0 else 1 - zh
        dst = rows_of(h, lax.rem(y + NY - d, NY), 1 - core)
        remote(dst, dst, cs.at[b, d], cr.at[b, d], img=partner).wait_recv()

    def a_copy(k, way):
        c = lax.rem(zl + FAR[k], NZ)
        src = part.at[c, lax.rem(x + 2, NX), pl.ds(way * 16, 16)]
        return remote(src, half_in.at[k, way], as_.at[k, way], ar.at[k, way], term=at_x((1, 3)[way]))

    def b_copy(k, way):
        c = lax.rem(zl + FAR[k], NZ)
        src = part.at[c, lax.rem(x + (1, 3)[way], NX)]
        return remote(src, full_in.at[k, way], bs.at[k, way], br.at[k, way], term=at_x((1, 3)[way]))

    def q_copy(k):
        c = lax.rem(zl + FAR[k], NZ)
        return remote(part.at[c, x], z_in.at[k], qs.at[k], qr.at[k], term=at_zl(c))

    def stage_a(k):
        for way in (0, 1):
            a_copy(k, way).start()

    def stage_b(k):
        c = lax.rem(zl + FAR[k], NZ)
        for way in (0, 1):
            a_copy(k, way).wait_recv()
            to = lax.rem(x + (1, 3)[way], NX)
            rows = slice(way * 16, way * 16 + 16)
            part[c, to, rows, :] = part[c, to, rows, :] + half_in[k, way]
            b_copy(k, way).start()

    def stage_c(k):
        c = lax.rem(zl + FAR[k], NZ)
        for way in (0, 1):
            b_copy(k, way).wait_recv()
        part[c, x] = part[c, x] + (full_in[k, 0] + full_in[k, 1])
        if FAR[k]:
            q_copy(k).start()

    @pl.when(zl < NZ - 1)
    def _():
        z_right(pat_ref, zl).start()

    @pl.when(zl > 0)
    def _():
        z_left(pat_ref, zl).start()

    for way in (0, 1):
        relay_send(way).start()
    spread(pat_ref, zl)
    for d in range(1, NY):
        y_send(0, d).start()
    c_send(0, 0).start()
    stage_a(0)

    feats[x, zl] = pat_ref[...]
    weight[pl.ds(pl.multiple_of(img * 64, 64), 64), :] = wt_ref[...]
    depth = weight.shape[0] - EXTRA
    top = lax.broadcasted_iota(jnp.int32, (EXTRA, width), 0) == 0
    weight[depth:, :] = jnp.where(top, MASKED, 0.0).astype(jnp.bfloat16)

    for s in range(1, NZ):
        if s == 1:
            pass_on(zl)
        else:
            @pl.when(zl >= s - 1)
            def _():
                pass_on(zl - (s - 1))

            @pl.when(zl + s - 1 < NZ)
            def _():
                pass_on(zl + s - 1)

        @pl.when(zl >= s)
        def _():
            o = zl - s
            remote(feats.at[x, o], feats.at[x, o], zs.at[0, o], zr.at[o], term=at_x(1)).wait_recv()

            @pl.when(zl < NZ - 1)
            def _():
                z_right(feats.at[x, o], o).start()

            spread(feats.at[x, o], o)

        @pl.when(zl + s < NZ)
        def _():
            o = zl + s
            remote(feats.at[x, o], feats.at[x, o], zs.at[1, o], zr.at[o], term=at_x(1)).wait_recv()

            @pl.when(zl > 0)
            def _():
                z_left(feats.at[x, o], o).start()

            spread(feats.at[x, o], o)

        if s == 2:
            for way in (0, 1):
                relay_send(way).wait_recv()
                relay_on(way).start()
        if s == 4:
            for way in (0, 1):
                relay_take(way)
            for d in range(1, NY):
                y_send(1, d).start()
            c_send(1, 0).start()
        if s in (3, 5, 6):
            d = {3: 1, 5: 2, 6: 3}[s]
            y_take(0, d)
            c_send(0, d).start()
        chunk(s)
        stage_a(s)
        stage_b(s - 1)
        if s >= 2:
            stage_c(s - 2)

    @pl.when(zl >= NZ - 1)
    def _():
        pass_on(0)

    @pl.when(zl <= 0)
    def _():
        pass_on(NZ - 1)

    for d in range(1, NY):
        y_take(1, d)
        c_send(1, d).start()
    stage_b(NZ - 1)
    stage_c(NZ - 2)
    for b in (0, 1):
        for d in range(NY):
            c_take(b, d)
    for o in range(NZ):
        for way in (0, 1):
            half_take(o, way)

    runmax[...] = jnp.full(runmax.shape, MASKED, jnp.float32)

    def group(g, carry):
        rows = feats[g].reshape(NZ * 32, feats.shape[3])
        logits = jnp.dot(rows, weight[...], preferred_element_type=jnp.float32)
        runmax[...] = jnp.maximum(runmax[...], jnp.max(logits.reshape(NZ, 32, width), axis=0))
        return carry

    lax.fori_loop(0, NX, group, 0)
    best = jnp.max(runmax[...].reshape(4, 8, width), axis=1)
    best = jnp.log1p(jnp.maximum(best + bias_ref[...], 0.0)).astype(jnp.bfloat16)
    best = jnp.concatenate([best, jnp.zeros_like(best)], axis=0)
    fresh[...] = lax.dot_general(
        best, dense[...], (((1,), (1,)), ((), ())), preferred_element_type=jnp.float32
    )

    def tx_copy(d):
        return remote(fresh, fresh_x.at[d - 1], tx_s.at[d - 1], tx_r.at[d - 1], term=at_x(d))

    def tz_copy(d):
        to = lax.rem(zl + d, NZ)
        return remote(fresh_z.at[to], fresh_in.at[d - 1], tz_s.at[d - 1], tz_r.at[d - 1], term=at_zl(to))

    for d in range(1, NX):
        tx_copy(d).start()
    stage_c(NZ - 1)
    for d in range(1, NX):
        tx_copy(d).wait_recv()
    total = fresh[...] + fresh_x[0] + fresh_x[1] + fresh_x[2]
    for k in range(NZ):
        fresh_z[k] = total[:, k * 128 : (k + 1) * 128]
    for d in range(1, NZ):
        tz_copy(d).start()
    result = part[zl, x]
    for k in range(NZ - 1):
        q_copy(k).wait_recv()
        result = result + z_in[k]
    main_ref[...] = result
    total = fresh_z[zl]
    for d in range(1, NZ):
        tz_copy(d).wait_recv()
        total = total + fresh_in[d - 1]
    new_ref[...] = total

    for o in range(NZ):
        @pl.when(jnp.logical_and(zl < NZ - 1, o <= zl))
        def _():
            z_right(feats.at[x, o], o).wait_send()

        @pl.when(jnp.logical_and(zl > 0, o >= zl))
        def _():
            z_left(feats.at[x, o], o).wait_send()

        for way in (0, 1):
            x_send(feats.at[x, o], o, way).wait_send()
            x_forward(o, way).wait_send()
    for way in (0, 1):
        relay_send(way).wait_send()
        relay_on(way).wait_send()
    for b in (0, 1):
        for d in range(1, NY):
            y_send(b, d).wait_send()
        for d in range(NY):
            c_send(b, d).wait_send()
    for k in range(NZ):
        for way in (0, 1):
            a_copy(k, way).wait_send()
            b_copy(k, way).wait_send()
        if FAR[k]:
            q_copy(k).wait_send()
    for d in range(1, NX):
        tx_copy(d).wait_send()
    for d in range(1, NZ):
        tz_copy(d).wait_send()


def shards(patches, patch_mask, proj_weight, proj_bias, slab, query_ids, term_weights):
    images, chunk, depth = patches.shape
    rows = images * chunk
    width = proj_weight.shape[1]
    masked = (1 - patch_mask.reshape(rows, 1)).astype(jnp.bfloat16)
    block = jnp.concatenate(
        [patches.reshape(rows, depth), jnp.pad(masked, ((0, 0), (0, EXTRA - 1)))], axis=1
    )
    queries = query_ids.shape[0]
    f32, b16 = jnp.float32, jnp.bfloat16
    dma = pltpu.SemaphoreType.DMA
    vmem = pl.BlockSpec(memory_space=pltpu.VMEM)
    main, new = pl.pallas_call(
        kernel,
        out_shape=(jax.ShapeDtypeStruct((32, 512), f32), jax.ShapeDtypeStruct((8, 128), f32)),
        in_specs=[vmem] * 6,
        out_specs=(vmem, vmem),
        scratch_shapes=[
            pltpu.VMEM((NX, NZ, rows, depth + EXTRA), b16),
            pltpu.VMEM((depth + EXTRA, width), b16),
            pltpu.VMEM((queries, width), b16),
            pltpu.VMEM((NZ, NX, 32, 512), f32),
            pltpu.VMEM((NZ, 2, 16, 512), f32),
            pltpu.VMEM((NZ, 2, 32, 512), f32),
            pltpu.VMEM((NZ - 1, 32, 512), f32),
            pltpu.VMEM((2, 32, width), b16),
            pltpu.VMEM((rows, width), f32),
            pltpu.VMEM((8, queries), f32),
            pltpu.VMEM((NX - 1, 8, queries), f32),
            pltpu.VMEM((NZ, 8, 128), f32),
            pltpu.VMEM((NZ - 1, 8, 128), f32),
            dma((2, NZ)), dma((NZ,)), dma((2, NZ)), dma((2, NZ)), dma((2, NZ)), dma((2, NZ)),
            dma((2,)), dma((2,)), dma((2,)), dma((2,)),
            dma((2, NY - 1)), dma((2, NY - 1)), dma((2, NY)), dma((2, NY)),
            dma((NZ, 2)), dma((NZ, 2)), dma((NZ, 2)), dma((NZ, 2)), dma((NZ - 1,)), dma((NZ - 1,)),
            dma((NX - 1,)), dma((NX - 1,)), dma((NZ - 1,)), dma((NZ - 1,)),
        ],
        compiler_params=pltpu.CompilerParams(
            collective_id=0, has_side_effects=True, vmem_limit_bytes=60 * 1024 * 1024
        ),
        name="score",
    )(query_ids, term_weights, proj_bias.reshape(1, width), block, proj_weight, slab)
    mine = lax.rem(lax.axis_index("term"), NX)
    new = lax.dynamic_slice(new, (0, mine * 32), (images, 32))
    return jnp.concatenate([main[:, : slab.shape[0]], new.T], axis=1)


def solution(mesh):
    placed = (
        P("img", "term", None),
        P("img", "term"),
        P("img", "term"),
        P("term"),
        P("img", "term"),
        P(),
        P(),
    )
    return jax.shard_map(
        shards, mesh=mesh, in_specs=placed, out_specs=P("term", "img"), check_vma=False
    )
```

time: 582 us -> 93.3 us (0.16)
  waiting for transfers between devices: 408 us -> 0 us
  blocking collectives: 133 us -> 0 us
  Pallas kernels: 0 us -> 82.8 us
  other arithmetic: 19 us -> 3.71 us
  between operations: 13.2 us -> 0.03 us
  matrix products: 8.82 us -> 0 us
    reduce_scatter x1 -> x0, waiting for transfers between devices: 243 us -> none  [shards(): lax.psum_scatter(lax.dot_general(dense_rows, impacts, (((1,), (1,)), ((),...]
    all_gather x2 -> x0, waiting for transfers between devices: 163 us -> none  [the longest x1 163 us: shards(): features = lax.all_gather(patches, 'term', axis=1, tiled=True)]
    all_gather x1 -> x0, blocking collectives: 133 us -> none  [shards(): lax.all_gather(patch_mask.astype(jnp.bfloat16), 'term', axis=1, tiled=True)]
    pallas_call x0 -> x1, Pallas kernels: none -> 82.8 us  [shards(): pl.pallas_call(kernel, out_shape=(jax.ShapeDtypeStruct((32, 512), f32), j...]
    reduce_sum x1 -> x0, other arithmetic: 17.3 us -> none  [shards(): jnp.sum(jnp.where(query_ids[:, :, None] == columns[None, None, :], weight...]
    dot_general x2 -> x0, matrix products: 8.82 us -> none  [the longest x1 6.15 us: shards(): jnp.einsum('npd,dv->npv', features, proj_full, preferred_element_type=jnp...]
  transfers between devices with their start and end apart: 3 -> 0, of which waited for: 2 -> 0; matrix products, arithmetic and copies ran while one was open for 3% -> 0% of each run, Pallas kernels for 0% -> 0%
where the time goes in v1:
time: 93.3 us; the launch traced here: 91.6 us
  Pallas kernels  82.8 us (89%)
  local copies, waits for them, and re-layouts  5.06 us (5%)
  other arithmetic  3.71 us (4%)
    pallas_call x1, Pallas kernels, shards(): pl.pallas_call(kernel, out_shape=(jax.ShapeDtypeStruct((32, 512), f32), j...  82.8 us
    unnamed x9, local copies, waits for them, and re-layouts  4.81 us

profile of v1, /device:TPU:24, one launch (start us, length us, event | category | flops | bytes accessed | tf_op | source)
XLA Modules:
  0.0 91.6 jit_solution(11783316855249585663)
XLA Ops:
  0.0 0.0 copy-start.1
  0.0 0.0 copy-start
  0.0 2.0 %copy.9.ids_ref = s32[1024,32]{1,0:T(8,128)} copy(s32[1024,32]{0,1:T(8,128)} %param.12) | data formatting | bytes 262144 | tf_op args[5]
  2.0 0.0 copy-done.1
  2.0 0.8 copy.10.tw_ref
  2.9 0.7 subtract_convert_fusion
  3.5 0.1 convert_element_type.18
  3.6 1.5 %fusion.1.pat_ref = bf16[32,1152]{1,0:T(8,128)(2,1)} fusion(bf16[32,1]{1,0:T(8,128)(2,1)S(1)} %convert_element_type.18, bf16[32,1024]{1,0:T(8,128)(2,1)} %bitcast.5), kind=kLoop, calls=%fused_computation.2 | loop fusion | flops 221184 | bytes 139328 | tf_op jit(solution)/shard_map/concatenate | solution.py:380
  5.1 0.0 copy-done
  5.1 1.3 %copy.11.slab_ref = bf16[508,960]{1,0:T(8,128)(2,1)} copy(bf16[508,960]{0,1:T(8,128)(2,1)S(1)} %copy-done) | data formatting | bytes 1950720 | tf_op args[4]
  6.4 82.8 %score.1 = (f32[32,512]{1,0:T(8,128)}, f32[8,128]{1,0:T(8,128)}) custom-call(s32[1024,32]{1,0:T(8,128)} %copy.9.ids_ref, bf16[1024,32]{1,0:T(8,128)(2,1)} %copy.10.tw_ref, f32[1,960]{1,0:T(1,128)} %bitcast.7, bf16[32,1152]{1,0:T(8,128)(2,1)} %fusion.1.pat_ref, bf16[64,960]{1,0:T(8,128)(2,1)} %wt_ref.1, bf16[508,960]{1,0:T(8,128)(2,1)} %copy.11.slab_ref), custom_call_target="tpu_custom_call" | custom-call | tf_op jit(solution)/shard_map/score/pallas_call | solution.py:387
  89.2 0.0 copy-start.2
  89.3 0.7 copy-done.2
  89.9 0.1 dynamic-slice_bitcast_fusion
  90.0 0.1 copy.12
  90.1 1.5 %pad_maximum_fusion = f32[32,512]{1,0:T(8,128)} fusion(f32[32,4]{1,0:T(8,128)S(1)} %copy.12, f32[32,508]{1,0:T(8,128)} %bitcast.6), kind=kLoop, calls=%fused_computation.3 | loop fusion | flops 16384 | bytes 131072 | tf_op jit(solution)/shard_map/concatenate | solution.py:419
Async XLA Ops:
  0.0 2.0 %copy-start.1 = (bf16[1024,32]{0,1:T(8,128)(2,1)S(1)}, bf16[1024,32]{0,1:T(8,128)(2,1)}, u32[]{:S(2)}) copy-start(bf16[1024,32]{0,1:T(8,128)(2,1)} %param.13) | copy-start | bytes 196612
  0.0 5.1 %copy-start = (bf16[508,960]{0,1:T(8,128)(2,1)S(1)}, bf16[508,960]{0,1:T(8,128)(2,1)}, u32[]{:S(2)}) copy-start(bf16[508,960]{0,1:T(8,128)(2,1)} %param.11) | copy-start | bytes 2926084
  89.2 0.7 copy-start.2

commit v2 on v0

v2 whole, which is shorter than its diff:
```python
import functools

import jax
import jax.numpy as jnp
from jax import lax
from jax.experimental import pallas as pl
from jax.experimental.pallas import tpu as pltpu
from jax.sharding import PartitionSpec as P

MESH = pl.DeviceIdType.MESH
NX, NY, NZ, NH = 4, 4, 8, 2
EXTRA = 128
FAR = (4, 3, 5, 2, 6, 1, 7, 0)
ONWARD = {0: (1,), 1: (1,), 2: (1,), 3: (1,), 4: (1,), 5: (1,), 6: (1,)}
MASKED = -1e30
PLAN = (
    ("chunk", 1), ("shares", 0), ("arrive", 1), ("chunk", 2), ("shares", 1), ("relay",), ("pass", 0),
    ("arrive", 2), ("chunk", 3), ("shares", 2), ("pass", 1), ("arrive", 3), ("chunk", 4), ("shares", 3),
    ("pass", 2), ("arrive", 4), ("chunk", 5), ("other",), ("row", 1), ("row", 2), ("row", 3), ("pass", 3),
    ("arrive", 5), ("chunk", 6), ("pass", 4), ("arrive", 6), ("chunk", 7), ("pass", 5), ("arrive", 7),
    ("row2", 1), ("row2", 2), ("row2", 3), ("pass", 6), ("pass", 7), ("shares", 4), ("shares", 5),
    ("shares", 6), ("shares", 7), ("gather", 0), ("gather", 1), ("rows",), ("project", 0), ("project", 1),
    ("project", 3), ("project", 2), ("new",), ("gather", 2), ("gather", 3), ("gather", 4), ("new2",),
    ("gather", 5), ("gather", 6), ("gather", 7),
)


def remote(src, dst, send, recv, **where):
    return pltpu.make_async_remote_copy(
        src_ref=src, dst_ref=dst, send_sem=send, recv_sem=recv, device_id=where, device_id_type=MESH
    )


def kernel(
    ids_ref, tw_ref, mask_ref, bias_ref, pat_ref, wt_ref, slab_ref,
    out_ref,
    ids_v, tw_v, slab_v, tile_ids, tile_tw, feats, weight, dense, part, x_out, x_in, z_out, z_in, relay, runmax,
    fresh, fresh_x, fresh_z, fresh_in, turned,
    ls, zs, zr, xs, xr, hs, hr, rs, rr, ws, wr, ys, yr, cs, cr,
    as_, ar, qs, qr, tx_s, tx_r, tz_s, tz_r,
):
    img = lax.axis_index("img")
    term = lax.axis_index("term")
    core, y, zh = lax.rem(img, 2), lax.rem(lax.div(img, 2), NY), lax.div(img, 2 * NY)
    x, zl = lax.rem(term, NX), lax.div(term, NX)
    depth = weight.shape[0] - EXTRA
    width = weight.shape[1]
    stored = slab_v.shape[1]

    def at_x(d):
        return zl * NX + lax.rem(x + d, NX)

    def at_zl(k):
        return k * NX + x

    def at_y(d):
        return zh * 8 + lax.rem(y + d, NY) * 2 + core

    def at_z(d):
        far = lax.rem(zh * NZ + zl + d, NH * NZ)
        return {"img": lax.div(far, NZ) * 8 + y * 2 + core, "term": lax.rem(far, NZ) * NX + x}

    partner = zh * 8 + y * 2 + 1 - core

    barrier = pltpu.get_barrier_semaphore()
    for hop in (4, 2, 1):
        for to in (zl + hop, zl - hop):
            @pl.when(jnp.logical_and(to >= 0, to < NZ))
            def _():
                pl.semaphore_signal(barrier, inc=1, device_id={"term": at_zl(to)}, device_id_type=MESH)
    pl.semaphore_signal(barrier, inc=1, device_id=at_z(jnp.where(zl < 4, 12, 4)), device_id_type=MESH)
    for d in range(1, NX):
        pl.semaphore_signal(barrier, inc=1, device_id={"term": at_x(d)}, device_id_type=MESH)
    for d in range(1, NY):
        pl.semaphore_signal(barrier, inc=1, device_id={"img": at_y(d)}, device_id_type=MESH)
    pl.semaphore_signal(barrier, inc=1, device_id={"img": partner}, device_id_type=MESH)
    near = 1 + jnp.where(jnp.logical_or(zl == 0, zl == NZ - 1), 1, 2) + jnp.where(
        jnp.logical_or(zl < 2, zl >= NZ - 2), 1, 2
    )

    own = weight.at[pl.ds(pl.multiple_of(img * 64, 64), 64)]
    local = [
        pltpu.make_async_copy(ids_ref, ids_v, ls.at[0]),
        pltpu.make_async_copy(tw_ref, tw_v, ls.at[1]),
        pltpu.make_async_copy(pat_ref, feats.at[x, zl, :, pl.ds(0, depth)], ls.at[2]),
        pltpu.make_async_copy(wt_ref, own, ls.at[3]),
        pltpu.make_async_copy(slab_ref, slab_v, ls.at[4]),
    ]
    for copy in local:
        copy.start()

    square = lax.broadcasted_iota(jnp.int32, (8, 8), 0) == lax.broadcasted_iota(jnp.int32, (8, 8), 1)
    off = []
    for n in range(mask_ref.shape[0]):
        row = jnp.broadcast_to(mask_ref[n : n + 1, :], (8, 8)).astype(jnp.float32)
        off.append(1.0 - jnp.sum(jnp.where(square, row, 0.0), axis=1, keepdims=True))
    off = jnp.concatenate(off, axis=0)
    lane = lax.broadcasted_iota(jnp.int32, (off.shape[0], EXTRA), 1)
    feats[x, zl, :, depth:] = jnp.where(lane == 0, off, 0.0).astype(jnp.bfloat16)
    top = lax.broadcasted_iota(jnp.int32, (EXTRA, width), 0) == 0
    weight[depth:, :] = jnp.where(top, MASKED, 0.0).astype(jnp.bfloat16)

    first = term * width
    local[0].wait()
    local[1].wait()

    def chunk(k):
        c = lax.rem(zl + FAR[k], NZ)
        slots = ids_v.shape[0]
        ids = (ids_v[:, pl.ds(pl.multiple_of(c * 128, 128), 128)] - first).astype(jnp.int16)
        tw = tw_v[:, pl.ds(pl.multiple_of(c * 128, 128), 128)]
        for j in range(slots):
            tile_ids[j] = jnp.broadcast_to(ids[j : j + 1, :], (16, 128))
            tile_tw[j] = jnp.broadcast_to(tw[j : j + 1, :], (16, 128))

        def band(r, carry):
            shape = (15, 16, 128)
            term_of = (
                lax.broadcasted_iota(jnp.int32, shape, 0) * 16 + lax.broadcasted_iota(jnp.int32, shape, 1) + r * 240
            ).astype(jnp.int16)
            acc = jnp.zeros(shape, jnp.bfloat16)
            for j in range(slots):
                acc = jnp.where(tile_ids[j][None] == term_of, tile_tw[j][None], acc)
            dense[c, pl.ds(pl.multiple_of(r * 240, 240), 240), :] = acc.reshape(240, 128)
            return carry

        lax.fori_loop(0, width // 240, band, 0)
        if k == 0:
            local[4].wait()
        share = lax.dot_general(
            dense[c], slab_v[...], (((0,), (0,)), ((), ())), preferred_element_type=jnp.float32
        )
        for d in range(NX):
            part[c, d, :, 384:512] = jnp.zeros((32, 128), jnp.float32)
            part[c, d, :, 0:stored] = share[d * 32 : (d + 1) * 32, :]

    chunk(0)
    local[2].wait()
    local[3].wait()
    pl.semaphore_wait(barrier, near + 8)

    def half(owner, o, h):
        return feats.at[owner, o, pl.ds(h * 16, 16)]

    def z_send(o, way, hop, h):
        to = zl + hop if way == 0 else zl - hop
        return remote(half(x, o, h), half(x, o, h), zs.at[way, o, hop // 2, h], zr.at[o, h], term=at_zl(to))

    def z_onward(o, k, way, h, finish=False):
        for hop in ONWARD.get(k, ()):
            @pl.when(zl + hop < NZ if way == 0 else zl >= hop)
            def _():
                copy = z_send(o, way, hop, h)
                copy.wait_send() if finish else copy.start()

    def x_send(o, way, h):
        return remote(half(x, o, h), half(x, o, h), xs.at[way, o, h], xr.at[way, o, h], term=at_x((1, 3)[way]))

    def x_forward(o, way):
        rows = half(lax.rem(x + (3, 1)[way], NX), o, way)
        return remote(rows, rows, hs.at[way, o], hr.at[way, o], term=at_x((1, 3)[way]))

    def x_take(o, way, h):
        rows = half(lax.rem(x + (3, 1)[way], NX), o, h)
        remote(rows, rows, xs.at[way, o, h], xr.at[way, o, h], term=at_x((1, 3)[way])).wait_recv()

    def half_take(o, way):
        rows = half(lax.rem(x + 2, NX), o, way)
        remote(rows, rows, hs.at[way, o], hr.at[way, o], term=at_x((1, 3)[way])).wait_recv()

    def sides(k, act):
        @pl.when(zl >= k)
        def _():
            act(zl - k, 0)

        @pl.when(zl + k < NZ)
        def _():
            act(zl + k, 1)

    def arrive(k):
        def act(o, way):
            for h in (0, 1):
                z_send(o, way, 1, h).wait_recv()
                z_onward(o, k, way, h)
                x_send(o, h, h).start()
                x_send(o, 1 - h, h).start()

        sides(k, act)

    def pass_on(k):
        def act(o, way):
            for turn in (0, 1):
                x_take(o, turn, turn)
                x_forward(o, turn).start()

        act(zl, 0) if k == 0 else sides(k, act)

    def rows_of(h, yy, cc, lo=0, n=64):
        return weight.at[pl.ds(pl.multiple_of((h * 8 + yy * 2 + cc) * 64 + lo, 32), n)]

    def relay_send(way):
        return remote(rows_of(zh, y, core, way * 32, 32), relay.at[way], rs.at[way], rr.at[way], **at_z((4, 12)[way]))

    def relay_on(way):
        far = at_z((4, 12)[way])
        h = lax.div(far["img"], 8)
        dst = rows_of(1 - h, y, core, way * 32, 32)
        return remote(relay.at[way], dst, ws.at[way], wr.at[way], **far)

    def relay_take(way):
        far = at_z((4, 12)[way])
        dst = rows_of(1 - zh, y, core, way * 32, 32)
        remote(relay.at[way], dst, ws.at[way], wr.at[way], **far).wait_recv()

    def y_send(b, d):
        rows = rows_of(zh if b == 0 else 1 - zh, y, core)
        return remote(rows, rows, ys.at[b, d - 1], yr.at[b, d - 1], img=at_y(d))

    def y_take(b, d):
        h = zh if b == 0 else 1 - zh
        dst = rows_of(h, lax.rem(y + NY - d, NY), core)
        remote(dst, dst, ys.at[b, d - 1], yr.at[b, d - 1], img=at_y(d)).wait_recv()

    def c_send(b, d):
        h = zh if b == 0 else 1 - zh
        rows = rows_of(h, lax.rem(y + NY - d, NY), core)
        return remote(rows, rows, cs.at[b, d], cr.at[b, d], img=partner)

    def c_take(b, d):
        h = zh if b == 0 else 1 - zh
        dst = rows_of(h, lax.rem(y + NY - d, NY), 1 - core)
        remote(dst, dst, cs.at[b, d], cr.at[b, d], img=partner).wait_recv()

    pos = lax.broadcasted_iota(jnp.int32, (32, 512), 1)

    def encode(v):
        v = jnp.where(pos < stored, v, 0.0)
        top = jnp.max(v, axis=1, keepdims=True)
        power = jnp.ceil(jnp.log2(jnp.maximum(top, 2.0**-100)))
        code = jnp.minimum((v * (jnp.exp2(-power) * 65535.0) + 0.5).astype(jnp.int32), 65535) - 32768
        return jnp.where(pos == stored, power.astype(jnp.int32), code).astype(jnp.int16)

    def decode(code):
        code = code.astype(jnp.int32)
        step = jnp.exp2(code[:, stored : stored + 1].astype(jnp.float32)) * (1.0 / 65535.0)
        return (code + 32768).astype(jnp.float32) * step

    def share_copy(k, d):
        return remote(x_out.at[k, d - 1], x_in.at[k, d - 1], as_.at[k, d - 1], ar.at[k, d - 1], term=at_x(d))

    def q_copy(k):
        c = lax.rem(zl + FAR[k], NZ)
        return remote(z_out.at[k], z_in.at[k], qs.at[k], qr.at[k], term=at_zl(c))

    def shares(k):
        c = lax.rem(zl + FAR[k], NZ)
        for d in (2, 1, 3):
            x_out[k, d - 1] = encode(part[c, lax.rem(x + d, NX)])
            share_copy(k, d).start()

    def gather_shares(k):
        c = lax.rem(zl + FAR[k], NZ)
        total = part[c, x]
        for d in range(1, NX):
            share_copy(k, d).wait_recv()
            total = total + decode(x_in[k, d - 1])
        if FAR[k]:
            z_out[k] = encode(total)
            q_copy(k).start()
        else:
            part[c, x] = total

    for way in (0, 1):
        relay_send(way).start()
    for h in (0, 1):
        for way in (0, 1):
            z_onward(zl, 0, way, h)
    for h in (0, 1):
        x_send(zl, h, h).start()
        x_send(zl, 1 - h, h).start()
    for d in range(1, NY):
        y_send(0, d).start()
    c_send(0, 0).start()

    def relayed():
        for way in (0, 1):
            relay_send(way).wait_recv()
            relay_on(way).start()

    def other_half():
        for way in (0, 1):
            relay_take(way)
        for d in range(1, NY):
            y_send(1, d).start()
        c_send(1, 0).start()

    def to_partner(b, d):
        y_take(b, d)
        c_send(b, d).start()

    def project(d):
        for o in range(NZ):
            if d == 2:
                half_take(o, 0)
                half_take(o, 1)
            elif d == 3:
                x_take(o, 0, 1)
            elif d == 1:
                x_take(o, 1, 0)
        rows = feats[lax.rem(x + d, NX)].reshape(NZ * 32, feats.shape[3])
        logits = jnp.dot(rows, weight[...], preferred_element_type=jnp.float32)
        best = jnp.max(logits.reshape(NZ, 32, width), axis=0)
        runmax[...] = best if d == 0 else jnp.maximum(runmax[...], best)

    def impacts():
        best = jnp.max(runmax[...].reshape(4, 8, width), axis=1)
        best = jnp.log1p(jnp.maximum(best + bias_ref[...], 0.0)).astype(jnp.bfloat16)
        best = jnp.concatenate([best, jnp.zeros_like(best)], axis=0)
        for k in range(NZ):
            fresh[k] = jnp.dot(best, dense[k], preferred_element_type=jnp.float32)
        for d in range(1, NX):
            tx_copy(d).start()

    def tx_copy(d):
        return remote(fresh, fresh_x.at[d - 1], tx_s.at[d - 1], tx_r.at[d - 1], term=at_x(d))

    def tz_copy(d):
        to = lax.rem(zl + d, NZ)
        return remote(fresh_z.at[to], fresh_in.at[d - 1], tz_s.at[d - 1], tz_r.at[d - 1], term=at_zl(to))

    def out_along_z():
        for d in range(1, NX):
            tx_copy(d).wait_recv()
        fresh_z[...] = fresh[...] + (fresh_x[0] + fresh_x[1] + fresh_x[2])
        for d in range(1, NZ):
            tz_copy(d).start()

    def rows_there():
        for b in (0, 1):
            for d in range(NY):
                c_take(b, d)

    acts = {
        "arrive": arrive, "pass": pass_on, "relay": relayed, "other": other_half,
        "row": lambda d: to_partner(0, d), "row2": lambda d: to_partner(1, d),
        "chunk": chunk, "shares": shares, "gather": gather_shares, "rows": rows_there, "project": project,
        "new": impacts, "new2": out_along_z,
    }
    for name, *at in PLAN:
        acts[name](*at)
    for k in ONWARD:
        for h in (0, 1):
            if k == 0:
                z_onward(zl, 0, 0, h, True)
                z_onward(zl, 0, 1, h, True)
            else:
                sides(k, lambda o, way: z_onward(o, k, way, h, True))
    for o in range(NZ):
        for way in (0, 1):
            x_send(o, way, 0).wait_send()
            x_send(o, way, 1).wait_send()
            x_forward(o, way).wait_send()
    for way in (0, 1):
        relay_send(way).wait_send()
        relay_on(way).wait_send()
    for b in (0, 1):
        for d in range(1, NY):
            y_send(b, d).wait_send()
        for d in range(NY):
            c_send(b, d).wait_send()
    for k in range(NZ):
        for d in range(1, NX):
            share_copy(k, d).wait_send()
        if FAR[k]:
            q_copy(k).wait_send()
    for d in range(1, NX):
        tx_copy(d).wait_send()
    for d in range(1, NZ):
        tz_copy(d).wait_send()

    result = part[zl, x]
    for k in range(NZ - 1):
        q_copy(k).wait_recv()
        result = result + decode(z_in[k])
    out_ref[...] = result

    total = fresh_z[zl]
    for d in range(1, NZ):
        tz_copy(d).wait_recv()
        total = total + fresh_in[d - 1]
    turned[...] = jnp.concatenate([total, jnp.zeros((120, 128), jnp.float32)], axis=0).T
    mine = pltpu.roll(turned[pl.ds(pl.multiple_of(x * 32, 32), 32), :], stored % 128, 1)
    lane = lax.broadcasted_iota(jnp.int32, (32, 128), 1)
    last = out_ref[:, 384:512]
    out_ref[:, 384:512] = jnp.where(lane >= stored % 128, mine, last)


def shards(patches, patch_mask, proj_weight, proj_bias, slab, query_ids, term_weights):
    images, chunk, depth = patches.shape
    rows = images * chunk
    width = proj_weight.shape[1]
    queries, slots = query_ids.shape
    stored = slab.shape[0]
    f32, b16, i16 = jnp.float32, jnp.bfloat16, jnp.int16
    dma = pltpu.SemaphoreType.DMA
    vmem = pl.BlockSpec(memory_space=pltpu.VMEM)
    hbm = pl.BlockSpec(memory_space=pl.ANY)
    return pl.pallas_call(
        kernel,
        out_shape=jax.ShapeDtypeStruct((32, 512), f32),
        in_specs=[hbm, hbm, vmem, vmem, hbm, hbm, hbm],
        out_specs=vmem,
        scratch_shapes=[
            pltpu.VMEM((slots, queries), jnp.int32),
            pltpu.VMEM((slots, queries), b16),
            pltpu.VMEM((width, stored), b16),
            pltpu.VMEM((slots, 16, 128), i16),
            pltpu.VMEM((slots, 16, 128), b16),
            pltpu.VMEM((NX, NZ, rows, depth + EXTRA), b16),
            pltpu.VMEM((depth + EXTRA, width), b16),
            pltpu.VMEM((NZ, width, 128), b16),
            pltpu.VMEM((NZ, NX, 32, 512), f32),
            pltpu.VMEM((NZ, NX - 1, 32, 512), i16),
            pltpu.VMEM((NZ, NX - 1, 32, 512), i16),
            pltpu.VMEM((NZ - 1, 32, 512), i16),
            pltpu.VMEM((NZ - 1, 32, 512), i16),
            pltpu.VMEM((2, 32, width), b16),
            pltpu.VMEM((rows, width), f32),
            pltpu.VMEM((NZ, 8, 128), f32),
            pltpu.VMEM((NX - 1, NZ, 8, 128), f32),
            pltpu.VMEM((NZ, 8, 128), f32),
            pltpu.VMEM((NZ - 1, 8, 128), f32),
            pltpu.VMEM((128, 128), f32),
            dma((5,)),
            dma((2, NZ, 3, 2)), dma((NZ, 2)), dma((2, NZ, 2)), dma((2, NZ, 2)), dma((2, NZ)), dma((2, NZ)),
            dma((2,)), dma((2,)), dma((2,)), dma((2,)),
            dma((2, NY - 1)), dma((2, NY - 1)), dma((2, NY)), dma((2, NY)),
            dma((NZ, NX - 1)), dma((NZ, NX - 1)), dma((NZ - 1,)), dma((NZ - 1,)),
            dma((NX - 1,)), dma((NX - 1,)), dma((NZ - 1,)), dma((NZ - 1,)),
        ],
        compiler_params=pltpu.CompilerParams(
            collective_id=0, has_side_effects=True, vmem_limit_bytes=60 * 1024 * 1024
        ),
        name="score",
    )(
        query_ids.T, term_weights.T, patch_mask, proj_bias.reshape(1, width), patches.reshape(rows, depth),
        proj_weight, slab.T,
    )


def solution(mesh):
    placed = (
        P("img", "term", None),
        P("img", "term"),
        P("img", "term"),
        P("term"),
        P("img", "term"),
        P(),
        P(),
    )
    return jax.shard_map(
        shards, mesh=mesh, in_specs=placed, out_specs=P("term", "img"), check_vma=False
    )
```

time: 582 us -> 70.7 us (0.12)
  waiting for transfers between devices: 408 us -> 0 us
  blocking collectives: 133 us -> 0 us
  Pallas kernels: 0 us -> 69 us
  other arithmetic: 19 us -> 0 us
  between operations: 13.2 us -> 0.01 us
  matrix products: 8.82 us -> 0 us
    reduce_scatter x1 -> x0, waiting for transfers between devices: 243 us -> none  [shards(): lax.psum_scatter(lax.dot_general(dense_rows, impacts, (((1,), (1,)), ((),...]
    all_gather x2 -> x0, waiting for transfers between devices: 163 us -> none  [the longest x1 163 us: shards(): features = lax.all_gather(patches, 'term', axis=1, tiled=True)]
    all_gather x1 -> x0, blocking collectives: 133 us -> none  [shards(): lax.all_gather(patch_mask.astype(jnp.bfloat16), 'term', axis=1, tiled=True)]
    pallas_call x0 -> x1, Pallas kernels: none -> 69 us  [shards(): pl.pallas_call(kernel, out_shape=jax.ShapeDtypeStruct((32, 512), f32), in...]
    reduce_sum x1 -> x0, other arithmetic: 17.3 us -> none  [shards(): jnp.sum(jnp.where(query_ids[:, :, None] == columns[None, None, :], weight...]
    dot_general x2 -> x0, matrix products: 8.82 us -> none  [the longest x1 6.15 us: shards(): jnp.einsum('npd,dv->npv', features, proj_full, preferred_element_type=jnp...]
  transfers between devices with their start and end apart: 3 -> 0, of which waited for: 2 -> 0; matrix products, arithmetic and copies ran while one was open for 3% -> 0% of each run, Pallas kernels for 0% -> 0%
where the time goes in v2:
time: 70.7 us; the launch traced here: 70.5 us
  Pallas kernels  69 us (98%)
  local copies, waits for them, and re-layouts  1.47 us (2%)
    pallas_call x1, Pallas kernels, shards(): pl.pallas_call(kernel, out_shape=jax.ShapeDtypeStruct((32, 512), f32), in...  69 us
    unnamed x1, local copies, waits for them, and re-layouts  1.47 us

profile of v2, /device:TPU:24, one launch (start us, length us, event | category | flops | bytes accessed | tf_op | source)
XLA Modules:
  0.0 70.5 jit_solution(14265182625813804049)
XLA Ops:
  0.0 69.0 %score.1 = f32[32,512]{1,0:T(8,128)} custom-call(s32[32,1024]{1,0:T(8,128)} %bitcast.6, bf16[32,1024]{1,0:T(8,128)(2,1)} %bitcast.7, s32[4,8]{1,0:T(4,128)} %mask_ref.1, f32[1,960]{1,0:T(1,128)} %bitcast.9, bf16[32,1024]{1,0:T(8,128)(2,1)} %bitcast.8, bf16[64,960]{1,0:T(8,128)(2,1)} %wt_ref.1, bf16[960,508]{1,0:T(8,128)(2,1)} %bitcast.5), custom_call_target="tpu_custom_call" | custom-call | tf_op jit(solution)/shard_map/score/pallas_call | solution.py:408
  69.0 1.5 %copy.9 = f32[32,512]{1,0:T(8,128)} copy(f32[32,512]{1,0:T(8,128)} %score.1) | data formatting | bytes 131072

commit v3 on v2

--- a/solution.py
+++ b/solution.py
@@ -14,14 +14,14 @@
 ONWARD = {0: (1,), 1: (1,), 2: (1,), 3: (1,), 4: (1,), 5: (1,), 6: (1,)}
 MASKED = -1e30
 PLAN = (
-    ("chunk", 1), ("shares", 0), ("arrive", 1), ("chunk", 2), ("shares", 1), ("relay",), ("pass", 0),
-    ("arrive", 2), ("chunk", 3), ("shares", 2), ("pass", 1), ("arrive", 3), ("chunk", 4), ("shares", 3),
-    ("pass", 2), ("arrive", 4), ("chunk", 5), ("other",), ("row", 1), ("row", 2), ("row", 3), ("pass", 3),
-    ("arrive", 5), ("chunk", 6), ("pass", 4), ("arrive", 6), ("chunk", 7), ("pass", 5), ("arrive", 7),
-    ("row2", 1), ("row2", 2), ("row2", 3), ("pass", 6), ("pass", 7), ("shares", 4), ("shares", 5),
-    ("shares", 6), ("shares", 7), ("gather", 0), ("gather", 1), ("rows",), ("project", 0), ("project", 1),
-    ("project", 3), ("project", 2), ("new",), ("gather", 2), ("gather", 3), ("gather", 4), ("new2",),
-    ("gather", 5), ("gather", 6), ("gather", 7),
+    ("chunk", 1), ("shares", 0), ("chunk", 2), ("shares", 1), ("chunk", 3), ("shares", 2), ("chunk", 4),
+    ("shares", 3), ("arrive", 1), ("relay",), ("pass", 0), ("chunk", 5), ("shares", 4), ("arrive", 2),
+    ("chunk", 6), ("shares", 5), ("pass", 1), ("arrive", 3), ("chunk", 7), ("shares", 6), ("shares", 7),
+    ("pass", 2), ("arrive", 4), ("other",), ("row", 1), ("row", 2), ("row", 3), ("arrive", 5), ("pass", 3),
+    ("arrive", 6), ("pass", 4), ("arrive", 7), ("pass", 5), ("row2", 1), ("row2", 2), ("row2", 3),
+    ("pass", 6), ("gather", 0), ("gather", 1), ("pass", 7), ("gather", 2), ("rows",), ("project", 0),
+    ("project", 1), ("gather", 3), ("project", 3), ("project", 2), ("new",), ("gather", 4), ("gather", 5),
+    ("new2",), ("gather", 6), ("gather", 7),
 )
 
 

time: 70.7 us -> 68.1 us (0.963)
  Pallas kernels: 69 us -> 66.4 us
    pallas_call x1, Pallas kernels: 69 us -> 66.4 us  [shards(): pl.pallas_call(kernel, out_shape=jax.ShapeDtypeStruct((32, 512), f32), in...]
where the time goes in v3:
time: 68.1 us; the launch traced here: 67.9 us
  Pallas kernels  66.4 us (98%)
  local copies, waits for them, and re-layouts  1.47 us (2%)
    pallas_call x1, Pallas kernels, shards(): pl.pallas_call(kernel, out_shape=jax.ShapeDtypeStruct((32, 512), f32), in...  66.4 us
    unnamed x1, local copies, waits for them, and re-layouts  1.47 us

profile of v3, /device:TPU:24, one launch (start us, length us, event | category | flops | bytes accessed | tf_op | source)
XLA Modules:
  0.0 67.9 jit_solution(4385085491284330545)
XLA Ops:
  0.0 66.4 %score.1 = f32[32,512]{1,0:T(8,128)} custom-call(s32[32,1024]{1,0:T(8,128)} %bitcast.6, bf16[32,1024]{1,0:T(8,128)(2,1)} %bitcast.7, s32[4,8]{1,0:T(4,128)} %mask_ref.1, f32[1,960]{1,0:T(1,128)} %bitcast.9, bf16[32,1024]{1,0:T(8,128)(2,1)} %bitcast.8, bf16[64,960]{1,0:T(8,128)(2,1)} %wt_ref.1, bf16[960,508]{1,0:T(8,128)(2,1)} %bitcast.5), custom_call_target="tpu_custom_call" | custom-call | tf_op jit(solution)/shard_map/score/pallas_call | solution.py:408
  66.4 1.5 %copy.9 = f32[32,512]{1,0:T(8,128)} copy(f32[32,512]{1,0:T(8,128)} %score.1) | data formatting | bytes 131072

commit v4 on v3

--- a/solution.py
+++ b/solution.py
@@ -9,10 +9,10 @@
 
 MESH = pl.DeviceIdType.MESH
 NX, NY, NZ, NH = 4, 4, 8, 2
-EXTRA = 128
 FAR = (4, 3, 5, 2, 6, 1, 7, 0)
 ONWARD = {0: (1,), 1: (1,), 2: (1,), 3: (1,), 4: (1,), 5: (1,), 6: (1,)}
 MASKED = -1e30
+PADDING = 64.0
 PLAN = (
     ("chunk", 1), ("shares", 0), ("chunk", 2), ("shares", 1), ("chunk", 3), ("shares", 2), ("chunk", 4),
     ("shares", 3), ("arrive", 1), ("relay",), ("pass", 0), ("chunk", 5), ("shares", 4), ("arrive", 2),
@@ -43,7 +43,6 @@
     term = lax.axis_index("term")
     core, y, zh = lax.rem(img, 2), lax.rem(lax.div(img, 2), NY), lax.div(img, 2 * NY)
     x, zl = lax.rem(term, NX), lax.div(term, NX)
-    depth = weight.shape[0] - EXTRA
     width = weight.shape[1]
     stored = slab_v.shape[1]
 
@@ -82,7 +81,7 @@
     local = [
         pltpu.make_async_copy(ids_ref, ids_v, ls.at[0]),
         pltpu.make_async_copy(tw_ref, tw_v, ls.at[1]),
-        pltpu.make_async_copy(pat_ref, feats.at[x, zl, :, pl.ds(0, depth)], ls.at[2]),
+        pltpu.make_async_copy(pat_ref, feats.at[x, zl], ls.at[2]),
         pltpu.make_async_copy(wt_ref, own, ls.at[3]),
         pltpu.make_async_copy(slab_ref, slab_v, ls.at[4]),
     ]
@@ -95,10 +94,6 @@
         row = jnp.broadcast_to(mask_ref[n : n + 1, :], (8, 8)).astype(jnp.float32)
         off.append(1.0 - jnp.sum(jnp.where(square, row, 0.0), axis=1, keepdims=True))
     off = jnp.concatenate(off, axis=0)
-    lane = lax.broadcasted_iota(jnp.int32, (off.shape[0], EXTRA), 1)
-    feats[x, zl, :, depth:] = jnp.where(lane == 0, off, 0.0).astype(jnp.bfloat16)
-    top = lax.broadcasted_iota(jnp.int32, (EXTRA, width), 0) == 0
-    weight[depth:, :] = jnp.where(top, MASKED, 0.0).astype(jnp.bfloat16)
 
     first = term * width
     local[0].wait()
@@ -136,6 +131,7 @@
 
     chunk(0)
     local[2].wait()
+    feats[x, zl] = jnp.where(off > 0.5, PADDING, feats[x, zl].astype(jnp.float32)).astype(jnp.bfloat16)
     local[3].wait()
     pl.semaphore_wait(barrier, near + 8)
 
@@ -309,6 +305,8 @@
                 x_take(o, 1, 0)
         rows = feats[lax.rem(x + d, NX)].reshape(NZ * 32, feats.shape[3])
         logits = jnp.dot(rows, weight[...], preferred_element_type=jnp.float32)
+        padding = rows[:, 0:128].astype(jnp.float32)[:, 0:1] > 0.5 * PADDING
+        logits = logits + jnp.where(padding, MASKED, 0.0)
         best = jnp.max(logits.reshape(NZ, 32, width), axis=0)
         runmax[...] = best if d == 0 else jnp.maximum(runmax[...], best)
 
@@ -416,8 +414,8 @@
             pltpu.VMEM((width, stored), b16),
             pltpu.VMEM((slots, 16, 128), i16),
             pltpu.VMEM((slots, 16, 128), b16),
-            pltpu.VMEM((NX, NZ, rows, depth + EXTRA), b16),
-            pltpu.VMEM((depth + EXTRA, width), b16),
+            pltpu.VMEM((NX, NZ, rows, depth), b16),
+            pltpu.VMEM((depth, width), b16),
             pltpu.VMEM((NZ, width, 128), b16),
             pltpu.VMEM((NZ, NX, 32, 512), f32),
             pltpu.VMEM((NZ, NX - 1, 32, 512), i16),

time: 68.1 us -> 66.8 us (0.981)
  Pallas kernels: 66.4 us -> 65.1 us
    pallas_call x1, Pallas kernels: 66.4 us -> 65.1 us  [shards(): pl.pallas_call(kernel, out_shape=jax.ShapeDtypeStruct((32, 512), f32), in...]
where the time goes in v4:
time: 66.8 us; the launch traced here: 66.6 us
  Pallas kernels  65.1 us (97%)
  local copies, waits for them, and re-layouts  1.47 us (2%)
    pallas_call x1, Pallas kernels, shards(): pl.pallas_call(kernel, out_shape=jax.ShapeDtypeStruct((32, 512), f32), in...  65.1 us
    unnamed x1, local copies, waits for them, and re-layouts  1.47 us

profile of v4, /device:TPU:24, one launch (start us, length us, event | category | flops | bytes accessed | tf_op | source)
XLA Modules:
  0.0 66.6 jit_solution(4161278991985824826)
XLA Ops:
  0.0 65.1 %score.1 = f32[32,512]{1,0:T(8,128)} custom-call(s32[32,1024]{1,0:T(8,128)} %bitcast.6, bf16[32,1024]{1,0:T(8,128)(2,1)} %bitcast.7, s32[4,8]{1,0:T(4,128)} %mask_ref.1, f32[1,960]{1,0:T(1,128)} %bitcast.9, bf16[32,1024]{1,0:T(8,128)(2,1)} %bitcast.8, bf16[64,960]{1,0:T(8,128)(2,1)} %wt_ref.1, bf16[960,508]{1,0:T(8,128)(2,1)} %bitcast.5), custom_call_target="tpu_custom_call" | custom-call | tf_op jit(solution)/shard_map/score/pallas_call | solution.py:406
  65.1 1.5 %copy.9 = f32[32,512]{1,0:T(8,128)} copy(f32[32,512]{1,0:T(8,128)} %score.1) | data formatting | bytes 131072
